TPU v7x, 32 devices: a whole 2x2x4 slice. The times are simulated.
32 devices in a mesh: fsdp: 8 (over z, y), ep: 4 (over x, core).
Axes of the slice: x: 2, y: 2, z: 4, core: 2. Of those that a mesh axis runs over, the one named last changes fastest.
Arguments:
- tokens: bfloat16 [4096, 3072], P(('fsdp', 'ep')), may hold values from -6 to 6
- expert_ids: int32 [4096, 2], P(('fsdp', 'ep')), may hold values from 0 to 3, all different within a row; in each aligned block of 128 rows (0 to 127, 128 to 255, ...) at most 128 rows name the same one
- gates: float32 [4096, 2], P(('fsdp', 'ep')), may hold values from 0.2 to 1
- up_weight: bfloat16 [4, 3072, 768], P('ep', 'fsdp'), may hold values from -0.109375 to 0.109375
- down_weight: bfloat16 [4, 768, 3072], P('ep', 'fsdp'), may hold values from -0.21875 to 0.21875
- cotangent: bfloat16 [4096, 3072], P(('fsdp', 'ep')), may hold values from -6 to 6
Outputs:
- mixed: bfloat16 [4096, 3072], P(('fsdp', 'ep'))
- token_grad: bfloat16 [4096, 3072], P(('fsdp', 'ep'))
- up_grad: bfloat16 [4, 3072, 768], P('ep', 'fsdp')
- down_grad: bfloat16 [4, 768, 3072], P('ep', 'fsdp')
Inputs may be any that keep to these rules, and one draw needn't show every extreme that they name: `expert_ids`: each token names two different experts. Among the tokens of one device (aligned blocks of 128 tokens) no expert is named more than 128 times, and in some block one expert is named exactly 128 times.
All inputs are finite; a program needn't handle non-finite values.
Results may differ from a plain program's by a relative error of at most 0.012.
Values may be sent and summed in bfloat16 or wider, within the bound.
A program may use at most 128 MiB of HBM per device.

v0:
```python
import jax
import jax.numpy as jnp
from jax import lax
from jax.sharding import PartitionSpec as P


def gelu_parts(pre):
    root = 0.7978845608028654
    inner = root * (pre + 0.044715 * pre * pre * pre)
    tanh_val = jnp.tanh(inner)
    value = 0.5 * pre * (1.0 + tanh_val)
    slope = 0.5 * (1.0 + tanh_val) + 0.5 * pre * (1.0 - tanh_val * tanh_val) * root * (
        1.0 + 3.0 * 0.044715 * pre * pre
    )
    return (value, slope)


def contract_last(left, right):
    return lax.dot_general(
        left, right, (((1,), (1,)), ((), ())), preferred_element_type=jnp.float32
    )


def contract_first(left, right):
    return lax.dot_general(
        left, right, (((0,), (0,)), ((), ())), preferred_element_type=jnp.float32
    )


def body(tokens, expert_ids, gates, up_weight, down_weight, cotangent):
    n_ep = lax.axis_size("ep")
    f32 = jnp.float32
    bf16 = jnp.bfloat16
    chosen = expert_ids[:, :, None] == jnp.arange(n_ep, dtype=jnp.int32)[None, None, :]
    dense_gates = jnp.sum(jnp.where(chosen, gates[:, :, None], 0.0), axis=1)
    all_gates = lax.all_gather(dense_gates, "ep", axis=0, tiled=True)
    mine = lax.axis_index("ep") == jnp.arange(n_ep, dtype=jnp.int32)
    gate = jnp.sum(jnp.where(mine[None, :], all_gates, 0.0), axis=1, keepdims=True)
    rows = lax.all_gather(tokens, "ep", axis=0, tiled=True)
    up = lax.all_gather(up_weight, "fsdp", axis=1, tiled=True)[0]
    cot = lax.all_gather(cotangent, "ep", axis=0, tiled=True)
    down = lax.all_gather(down_weight, "fsdp", axis=1, tiled=True)[0]
    grad_rows = (cot.astype(f32) * gate).astype(bf16)
    pre = jnp.dot(rows, up, preferred_element_type=f32)
    value, slope = gelu_parts(pre)
    hidden = value.astype(bf16)
    down_grad = lax.psum_scatter(
        contract_first(hidden, grad_rows).astype(bf16), "fsdp", scatter_dimension=0, tiled=True
    )
    d_hidden = contract_last(grad_rows, down)
    d_pre = (d_hidden * slope).astype(bf16)
    up_grad = lax.psum_scatter(
        contract_first(rows, d_pre).astype(bf16), "fsdp", scatter_dimension=0, tiled=True
    )
    result = jnp.dot(hidden, down, preferred_element_type=f32)
    mixed = lax.psum_scatter((result * gate).astype(bf16), "ep", scatter_dimension=0, tiled=True)
    back = contract_last(d_pre, up).astype(bf16)
    token_grad = lax.psum_scatter(back, "ep", scatter_dimension=0, tiled=True)
    return (mixed, token_grad, up_grad[None], down_grad[None])


def solution(mesh):
    placed = (
        P(("fsdp", "ep"), None),
        P(("fsdp", "ep"), None),
        P(("fsdp", "ep"), None),
        P("ep", "fsdp", None),
        P("ep", "fsdp", None),
        P(("fsdp", "ep"), None),
    )
    return jax.shard_map(
        body,
        mesh=mesh,
        in_specs=placed,
        out_specs=(
            P(("fsdp", "ep"), None),
            P(("fsdp", "ep"), None),
            P("ep", "fsdp", None),
            P("ep", "fsdp", None),
        ),
        check_vma=False,
    )
```

profile of v0, /device:TPU:0, one launch (start us, length us, event | category | flops | bytes accessed | tf_op | source)
XLA Modules:
  0.0 534.1 jit_solution(15591842795536665031)
XLA Ops:
  7.2 0.0 copy-start
  7.2 0.0 copy-start.1
  7.2 0.0 all-gather.5.cloned.1.call-start
  7.2 0.7 all-gather.5.cloned.1.call-update
  7.9 0.0 all-gather.7.cloned.1.call-start
  8.0 0.7 all-gather.7.cloned.1.call-update
  8.7 0.0 all-gather.11.cloned.1.call-start
  8.7 0.7 all-gather.11.cloned.1.call-update
  9.4 0.0 all-gather.9.cloned.1.call-start
  9.5 0.5 all-gather.9.cloned.1.call-update
  10.0 0.0 reduce-scatter.13.cloned.1.call-start
  10.0 0.0 copy-done
  10.0 0.0 copy-done.1
  10.1 6.1 %all_gather.18 = f32[512,4]{0,1:T(4,128)S(1)} all-gather(f32[128,4]{0,1:T(4,128)S(1)} %select_reduce_fusion.1), channel_id=1, replica_groups=mesh['fsdp'=8,'ep'=4] {'ep'}, dimensions={0}, use_global_device_ids=true | all-gather | bytes 10240 | tf_op jit(solution)/shard_map/all_gather | solution.py:36
  16.2 0.1 select_reduce_fusion
  16.3 24.6 %all-gather.5.cloned.1.call-done = bf16[512,3072]{1,0:T(8,128)(2,1)} async-done(((bf16[128,3072]{1,0:T(8,128)(2,1)}), bf16[512,3072]{1,0:T(8,128)(2,1)}) %all-gather.5.cloned.1.call-update) | async-done | bytes 3145744 | tf_op jit(solution)/shard_map/all_gather | solution.py:39
  40.8 82.1 %all-gather.7.cloned.1.call-done = bf16[1,3072,768]{2,1,0:T(8,128)(2,1)} async-done(((bf16[1,384,768]{2,1,0:T(8,128)(2,1)}), bf16[1,3072,768]{2,1,0:T(8,128)(2,1)}) %all-gather.7.cloned.1.call-update) | async-done | bytes 4718608 | tf_op jit(solution)/shard_map/all_gather | solution.py:40
  122.9 7.1 %fusion.5 = f32[512,768]{1,0:T(8,128)} fusion(bf16[512,3072]{1,0:T(8,128)(2,1)} %all-gather.5.cloned.1.call-done, bf16[1,3072,768]{2,1,0:T(8,128)(2,1)} %all-gather.7.cloned.1.call-done), kind=kOutput, calls=%fused_computation.9 | convolution fusion | flops 2415919104 | bytes 9437184 | tf_op jit(solution)/shard_map/dot_general | solution.py:44
  130.0 0.0 copy-start.3
  130.0 21.2 %all-gather.11.cloned.1.call-done = bf16[512,3072]{1,0:T(8,128)(2,1)} async-done(((bf16[128,3072]{1,0:T(8,128)(2,1)}), bf16[512,3072]{1,0:T(8,128)(2,1)}) %all-gather.11.cloned.1.call-update) | async-done | bytes 3145744 | tf_op jit(solution)/shard_map/all_gather | solution.py:41
  151.2 82.0 %all-gather.9.cloned.1.call-done = bf16[1,768,3072]{2,1,0:T(8,128)(2,1)} async-done(((bf16[1,96,3072]{2,1,0:T(8,128)(2,1)}), bf16[1,768,3072]{2,1,0:T(8,128)(2,1)}) %all-gather.9.cloned.1.call-update) | async-done | bytes 4718608 | tf_op jit(solution)/shard_map/all_gather | solution.py:42
  233.2 7.0 %fusion.17 = bf16[512,768]{1,0:T(8,128)(2,1)S(1)} fusion(f32[512,768]{1,0:T(8,128)} %fusion.5, bf16[1,768,3072]{2,1,0:T(8,128)(2,1)} %all-gather.9.cloned.1.call-done, bf16[512,3072]{1,0:T(8,128)(2,1)} %all-gather.11.cloned.1.call-done, f32[512]{0:T(512)S(1)} %select_reduce_fusion), kind=kOutput, calls=%fused_computation.21 | convolution fusion | flops 2428108800 | bytes 10225664 | tf_op jit(solution)/shard_map/dot_general | solution.py:19
  240.2 0.0 copy-start.5
  240.2 0.9 copy-done.5
  241.1 0.0 copy-done.3
  241.1 4.3 fusion.7
  245.4 6.7 %copy.17 = bf16[3072,768]{1,0:T(8,128)(2,1)} copy(bf16[3072,768]{0,1:T(8,128)(2,1)} %fusion.7) | data formatting | bytes 9437184
  252.1 0.0 copy-start.4
  252.1 0.0 reduce-scatter.13.cloned.1.call-update
  252.2 0.0 reduce-scatter.7.cloned.1.call-start
  252.2 1.3 copy-done.4
  253.6 6.5 %multiply_convert_fusion.1 = bf16[512,3072]{1,0:T(8,128)(2,1)} fusion(bf16[1,768,3072]{2,1,0:T(8,128)(2,1)} %all-gather.9.cloned.1.call-done, f32[512]{0:T(512)S(1)} %select_reduce_fusion, f32[512,768]{1,0:T(8,128)S(1)} %copy-done.4), kind=kOutput, calls=%fused_computation.1 | convolution fusion | flops 2422603776 | bytes 9439232 | tf_op jit(solution)/shard_map/dot_general | solution.py:55
  260.0 0.0 copy-start.6
  260.0 0.0 reduce-scatter.7.cloned.1.call-update
  260.0 0.0 reduce-scatter.9.cloned.1.call-start
  260.1 1.1 copy-done.6
  261.1 6.4 %fusion.8 = bf16[512,3072]{1,0:T(8,128)(2,1)} fusion(bf16[512,768]{1,0:T(8,128)(2,1)S(1)} %copy-done.6, bf16[1,3072,768]{2,1,0:T(8,128)(2,1)} %all-gather.7.cloned.1.call-done), kind=kOutput, calls=%fused_computation.12 | convolution fusion | flops 2417491968 | bytes 8650752 | tf_op jit(solution)/shard_map/dot_general | solution.py:19
  267.5 0.0 copy-start.2
  267.5 0.0 reduce-scatter.9.cloned.1.call-update
  267.6 0.0 reduce-scatter.11.cloned.1.call-start
  267.6 1.8 copy-done.2
  269.5 6.5 %convolution_convert_fusion = bf16[768,3072]{1,0:T(8,128)(2,1)} fusion(bf16[512,3072]{1,0:T(8,128)(2,1)S(1)} %copy-done.2, f32[512]{0:T(512)S(1)} %select_reduce_fusion, f32[512,768]{1,0:T(8,128)} %fusion.5), kind=kOutput, calls=%fused_computation.2 | convolution fusion | flops 2426535936 | bytes 9439232 | tf_op jit(solution)/shard_map/dot_general | solution.py:25
  275.9 0.0 reduce-scatter.11.cloned.1.call-update
  276.0 69.8 %reduce-scatter.13.cloned.1.call-done = bf16[384,768]{1,0:T(8,128)(2,1)} async-done(((bf16[3072,768]{1,0:T(8,128)(2,1)}), bf16[384,768]{1,0:T(8,128)(2,1)}) %reduce-scatter.13.cloned.1.call-update) | async-done | bytes 589840
  345.7 1.4 copy.18
  347.1 1.1 copy.16
  348.2 38.3 %reduce-scatter.7.cloned.1.call-done = bf16[128,3072]{1,0:T(8,128)(2,1)} async-done(((bf16[512,3072]{1,0:T(8,128)(2,1)}), bf16[128,3072]{1,0:T(8,128)(2,1)}) %reduce-scatter.7.cloned.1.call-update) | async-done | bytes 786448 | tf_op jit(solution)/shard_map/reduce_scatter | solution.py:56
  386.4 41.2 %reduce-scatter.9.cloned.1.call-done = bf16[128,3072]{1,0:T(8,128)(2,1)} async-done(((bf16[512,3072]{1,0:T(8,128)(2,1)}), bf16[128,3072]{1,0:T(8,128)(2,1)}) %reduce-scatter.9.cloned.1.call-update) | async-done | bytes 786448 | tf_op jit(solution)/shard_map/reduce_scatter | solution.py:58
  427.6 99.7 %reduce-scatter.11.cloned.1.call-done = bf16[96,3072]{1,0:T(8,128)(2,1)} async-done(((bf16[768,3072]{1,0:T(8,128)(2,1)}), bf16[96,3072]{1,0:T(8,128)(2,1)}) %reduce-scatter.11.cloned.1.call-update) | async-done | bytes 589840 | tf_op jit(solution)/shard_map/reduce_scatter | solution.py:47
  (2 shorter events, 0.0 us)
Async XLA Ops:
  7.2 2.9 copy-start
  7.2 2.9 copy-start.1
  7.2 33.7 %all-gather.5.cloned.1.call-start = ((), (), s32[]{:S(2)}) async-start(), calls=%async_computation.4 | async-start | bytes 3932160 | tf_op jit(solution)/shard_map/all_gather | solution.py:39
  7.9 115.0 %all-gather.7.cloned.1.call-start = ((), (), s32[]{:S(2)}) async-start(), calls=%async_computation.5 | async-start | bytes 5308416 | tf_op jit(solution)/shard_map/all_gather | solution.py:40
  8.7 142.5 %all-gather.11.cloned.1.call-start = ((), (), s32[]{:S(2)}) async-start(), calls=%async_computation.8 | async-start | bytes 3932160 | tf_op jit(solution)/shard_map/all_gather | solution.py:41
  9.4 223.8 %all-gather.9.cloned.1.call-start = ((), (), s32[]{:S(2)}) async-start(), calls=%async_computation.6 | async-start | bytes 5308416 | tf_op jit(solution)/shard_map/all_gather | solution.py:42
  10.0 335.7 %reduce-scatter.13.cloned.1.call-start = ((), (), s32[]{:S(2)}) async-start(), calls=%async_computation.11 | async-start | bytes 5308416
  130.0 111.0 %copy-start.3 = (bf16[512,3072]{1,0:T(8,128)(2,1)S(1)}, bf16[512,3072]{1,0:T(8,128)(2,1)}, u32[]{:S(2)}) copy-start(bf16[512,3072]{1,0:T(8,128)(2,1)} %all-gather.5.cloned.1.call-done) | copy-start | bytes 9437188
  240.2 0.9 copy-start.5
  252.1 1.4 copy-start.4
  252.2 134.2 %reduce-scatter.7.cloned.1.call-start = ((), (), s32[]{:S(2)}) async-start(), calls=%async_computation.7 | async-start | bytes 3932160 | tf_op jit(solution)/shard_map/reduce_scatter | solution.py:56
  260.0 1.1 copy-start.6
  260.0 167.6 %reduce-scatter.9.cloned.1.call-start = ((), (), s32[]{:S(2)}) async-start(), calls=%async_computation.9 | async-start | bytes 3932160 | tf_op jit(solution)/shard_map/reduce_scatter | solution.py:58
  267.5 1.9 copy-start.2
  267.6 259.7 %reduce-scatter.11.cloned.1.call-start = ((), (), s32[]{:S(2)}) async-start(), calls=%async_computation.10 | async-start | bytes 5308416 | tf_op jit(solution)/shard_map/reduce_scatter | solution.py:47
Sparse Core Ops, SparseCore 0:
  9.6 31.2 all-gather.4
  43.0 79.8 all-gather.6
  124.5 26.6 all-gather.10
  153.3 79.8 all-gather.8
  252.3 93.3 reduce-scatter.12
  348.7 37.6 reduce-scatter.6
  389.7 37.9 reduce-scatter.8
  431.9 95.3 reduce-scatter.10
where the time goes:
time: 535 us; the launch traced here: 534 us
  waiting for transfers between devices  461 us (86%)
  matrix products  37.8 us (7%)
  local copies, waits for them, and re-layouts  14.3 us (3%)
  between operations  14.2 us (3%)
  blocking collectives  6.11 us (1%)
    reduce_scatter x1, waiting for transfers between devices, body(): lax.psum_scatter(contract_first(hidden, grad_rows).astype(bf16), 'fsdp',...  99.7 us
    all_gather x1, waiting for transfers between devices, body(): up = lax.all_gather(up_weight, 'fsdp', axis=1, tiled=True)[0]  82.1 us
    all_gather x1, waiting for transfers between devices, body(): down = lax.all_gather(down_weight, 'fsdp', axis=1, tiled=True)[0]  82 us
    unnamed x9, waiting for transfers between devices  72.4 us
    reduce_scatter x1, waiting for transfers between devices, body(): token_grad = lax.psum_scatter(back, 'ep', scatter_dimension=0, tiled=True)  41.2 us
    reduce_scatter x1, waiting for transfers between devices, body(): lax.psum_scatter((result * gate).astype(bf16), 'ep', scatter_dimension=0,...  38.3 us
    all_gather x1, waiting for transfers between devices, body(): rows = lax.all_gather(tokens, 'ep', axis=0, tiled=True)  24.6 us
    all_gather x1, waiting for transfers between devices, body(): cot = lax.all_gather(cotangent, 'ep', axis=0, tiled=True)  21.2 us
  transfers between devices with their start and end apart: 8, of which 8 were waited for; matrix products, arithmetic and copies ran while one was open for 5% of the time, Pallas kernels for 0%

commit v1 on v0

--- a/solution.py
+++ b/solution.py
@@ -2,6 +2,27 @@
 import jax.numpy as jnp
 from jax import lax
 from jax.sharding import PartitionSpec as P
+
+
+def gather_around(array, axis, dim):
+    peers, index, rows = (lax.axis_size(axis), lax.axis_index(axis), array.shape[dim])
+    right = [(i, (i + 1) % peers) for i in range(peers)]
+    backward = [(i, (i - 1) % peers) for i in range(peers)]
+    filled = jnp.zeros((*array.shape[:dim], peers * rows, *array.shape[dim + 1 :]), array.dtype)
+    filled = lax.dynamic_update_slice_in_dim(filled, array, index * rows, axis=dim)
+    from_left = from_right = array
+    half = peers // 2
+    for hop in range(1, half + 1):
+        from_left = lax.ppermute(from_left, axis, right)
+        filled = lax.dynamic_update_slice_in_dim(
+            filled, from_left, (index - hop) % peers * rows, axis=dim
+        )
+        if hop < peers - half:
+            from_right = lax.ppermute(from_right, axis, backward)
+            filled = lax.dynamic_update_slice_in_dim(
+                filled, from_right, (index + hop) % peers * rows, axis=dim
+            )
+    return filled
 
 
 def gelu_parts(pre):
@@ -36,7 +57,7 @@
     all_gates = lax.all_gather(dense_gates, "ep", axis=0, tiled=True)
     mine = lax.axis_index("ep") == jnp.arange(n_ep, dtype=jnp.int32)
     gate = jnp.sum(jnp.where(mine[None, :], all_gates, 0.0), axis=1, keepdims=True)
-    rows = lax.all_gather(tokens, "ep", axis=0, tiled=True)
+    rows = gather_around(tokens, "ep", 0)
     up = lax.all_gather(up_weight, "fsdp", axis=1, tiled=True)[0]
     cot = lax.all_gather(cotangent, "ep", axis=0, tiled=True)
     down = lax.all_gather(down_weight, "fsdp", axis=1, tiled=True)[0]

time: 535 us -> 489 us (0.914)
  waiting for transfers between devices: 461 us -> 408 us
  blocking collectives: 6.11 us -> 18.4 us
  local copies, waits for them, and re-layouts: 14.3 us -> 6.11 us
    reduce_scatter x0 -> x1, waiting for transfers between devices: none -> 99.5 us  [body(): lax.psum_scatter(contract_first(rows, d_pre).astype(bf16), 'fsdp', scatte...]
    unnamed x9 -> x7, waiting for transfers between devices: 72.4 us -> 2.12 us
    all_gather x1, waiting for transfers between devices: 82.1 us -> 49 us  [body(): up = lax.all_gather(up_weight, 'fsdp', axis=1, tiled=True)[0]]
    reduce_scatter x1, waiting for transfers between devices: 38.3 us -> 12.1 us  [body(): lax.psum_scatter((result * gate).astype(bf16), 'ep', scatter_dimension=0,...]
    all_gather x1 -> x0, waiting for transfers between devices: 24.6 us -> none  [body(): rows = lax.all_gather(tokens, 'ep', axis=0, tiled=True)]
    all_gather x1, blocking collectives: 6.11 us -> 18.4 us  [body(): all_gates = lax.all_gather(dense_gates, 'ep', axis=0, tiled=True)]
    unnamed x17 -> x6, local copies, waits for them, and re-layouts: 14.3 us -> 3.19 us
    ppermute x0 -> x3, waiting for transfers between devices: none -> 9.27 us  [the longest x2 9.26 us: gather_around(): from_left = lax.ppermute(from_left, axis, right)]
  transfers between devices with their start and end apart: 8 -> 10, of which waited for: 8 -> 8; matrix products, arithmetic and copies ran while one was open for 5% -> 9% of each run, Pallas kernels for 0% -> 0%
where the time goes in v1:
time: 489 us
  waiting for transfers between devices  408 us (83%)
  matrix products  38.8 us (8%)
  blocking collectives  18.4 us (4%)
  between operations  14.2 us (3%)
  local copies, waits for them, and re-layouts  6.11 us (1%)
    reduce_scatter x1, waiting for transfers between devices, body(): lax.psum_scatter(contract_first(rows, d_pre).astype(bf16), 'fsdp', scatte...  99.5 us
    reduce_scatter x1, waiting for transfers between devices, body(): lax.psum_scatter(contract_first(hidden, grad_rows).astype(bf16), 'fsdp',...  99.3 us
    all_gather x1, waiting for transfers between devices, body(): down = lax.all_gather(down_weight, 'fsdp', axis=1, tiled=True)[0]  74.1 us
    all_gather x1, waiting for transfers between devices, body(): up = lax.all_gather(up_weight, 'fsdp', axis=1, tiled=True)[0]  49 us
    reduce_scatter x1, waiting for transfers between devices, body(): token_grad = lax.psum_scatter(back, 'ep', scatter_dimension=0, tiled=True)  41.1 us
    all_gather x1, waiting for transfers between devices, body(): cot = lax.all_gather(cotangent, 'ep', axis=0, tiled=True)  21 us
    all_gather x1, blocking collectives, body(): all_gates = lax.all_gather(dense_gates, 'ep', axis=0, tiled=True)  18.4 us
    dot_general x2, matrix products, contract_last(): lax.dot_general(left, right, (((1,), (1,)), ((), ())), preferred_element_...  13.6 us
  transfers between devices with their start and end apart: 10, of which 8 were waited for; matrix products, arithmetic and copies ran while one was open for 9% of the time, Pallas kernels for 0%

profile of v1, /device:TPU:0, one launch (start us, length us, event | category | flops | bytes accessed | tf_op | source)
XLA Modules:
  0.0 489.0 jit_solution(11620797197155897777)
XLA Ops:
  7.2 0.0 all-gather.4.cloned.1.call-start
  7.2 0.7 all-gather.4.cloned.1.call-update
  7.9 0.0 all-gather.6.cloned.1.call-start
  7.9 0.7 all-gather.6.cloned.1.call-update
  8.6 0.0 all-gather.8.cloned.1.call-start
  8.7 0.7 all-gather.8.cloned.1.call-update
  9.4 0.0 reduce-scatter.5.cloned.1.call-start
  9.4 0.5 collective-permute-start
  9.9 2.0 collective-permute-start.1
  11.9 0.0 copy-start
  11.9 0.8 select_reduce_fusion.1
  12.7 18.4 %all_gather.14 = f32[512,4]{0,1:T(4,128)S(1)} all-gather(f32[128,4]{0,1:T(4,128)S(1)} %select_reduce_fusion.1), channel_id=1, replica_groups=mesh['fsdp'=8,'ep'=4] {'ep'}, dimensions={0}, use_global_device_ids=true | all-gather | bytes 10240 | tf_op jit(solution)/shard_map/all_gather | solution.py:57
  31.1 0.4 broadcast_in_dim.38
  31.5 0.0 copy-done
  31.5 0.1 constant_dynamic-update-slice_fusion.3
  31.6 0.0 collective-permute-done
  31.6 0.4 collective-permute-start.2
  31.9 0.1 select_reduce_fusion
  32.0 1.2 constant_dynamic-update-slice_fusion.2
  33.3 0.0 collective-permute-done.1
  33.3 1.2 constant_dynamic-update-slice_fusion.1
  34.5 9.3 %collective-permute-done.2 = bf16[128,3072]{1,0:T(8,128)(2,1)S(1)} collective-permute-done((bf16[128,3072]{1,0:T(8,128)(2,1)}, bf16[128,3072]{1,0:T(8,128)(2,1)S(1)}, u32[]{:S(2)}, u32[]{:S(2)}) %collective-permute-start.2) | collective-permute-done | bytes 786464 | tf_op jit(solution)/shard_map/ppermute | solution.py:16
  43.7 0.1 constant_dynamic-update-slice_fusion
  43.8 49.0 %all-gather.4.cloned.1.call-done = bf16[1,3072,768]{2,1,0:T(8,128)(2,1)} async-done(((bf16[1,384,768]{2,1,0:T(8,128)(2,1)}), bf16[1,3072,768]{2,1,0:T(8,128)(2,1)}) %all-gather.4.cloned.1.call-update) | async-done | bytes 4718608 | tf_op jit(solution)/shard_map/all_gather | solution.py:61
  92.8 6.1 %fusion.5 = f32[512,768]{1,0:T(8,128)} fusion(bf16[512,3072]{1,0:T(8,128)(2,1)S(1)} %constant_dynamic-update-slice_fusion, bf16[1,3072,768]{2,1,0:T(8,128)(2,1)} %all-gather.4.cloned.1.call-done), kind=kOutput, calls=%fused_computation.9 | convolution fusion | flops 2415919104 | bytes 9437184 | tf_op jit(solution)/shard_map/dot_general | solution.py:65
  98.9 74.1 %all-gather.6.cloned.1.call-done = bf16[1,768,3072]{2,1,0:T(8,128)(2,1)} async-done(((bf16[1,96,3072]{2,1,0:T(8,128)(2,1)}), bf16[1,768,3072]{2,1,0:T(8,128)(2,1)}) %all-gather.6.cloned.1.call-update) | async-done | bytes 4718608 | tf_op jit(solution)/shard_map/all_gather | solution.py:63
  173.0 7.2 %multiply_convert_fusion.1 = bf16[512,3072]{1,0:T(8,128)(2,1)} fusion(bf16[1,768,3072]{2,1,0:T(8,128)(2,1)} %all-gather.6.cloned.1.call-done, f32[512]{0:T(512)S(1)} %select_reduce_fusion, f32[512,768]{1,0:T(8,128)} %fusion.5), kind=kOutput, calls=%fused_computation.1 | convolution fusion | flops 2422603776 | bytes 9439232 | tf_op jit(solution)/shard_map/dot_general | solution.py:76
  180.2 0.0 reduce-scatter.5.cloned.1.call-update
  180.3 0.0 reduce-scatter.7.cloned.1.call-start
  180.3 21.0 %all-gather.8.cloned.1.call-done = bf16[512,3072]{1,0:T(8,128)(2,1)} async-done(((bf16[128,3072]{1,0:T(8,128)(2,1)}), bf16[512,3072]{1,0:T(8,128)(2,1)}) %all-gather.8.cloned.1.call-update) | async-done | bytes 3145744 | tf_op jit(solution)/shard_map/all_gather | solution.py:62
  201.3 7.0 %fusion.16 = bf16[512,768]{1,0:T(8,128)(2,1)S(1)} fusion(f32[512,768]{1,0:T(8,128)} %fusion.5, bf16[1,768,3072]{2,1,0:T(8,128)(2,1)} %all-gather.6.cloned.1.call-done, bf16[512,3072]{1,0:T(8,128)(2,1)} %all-gather.8.cloned.1.call-done, f32[512]{0:T(512)S(1)} %select_reduce_fusion), kind=kOutput, calls=%fused_computation.20 | convolution fusion | flops 2428108800 | bytes 10225664 | tf_op jit(solution)/shard_map/dot_general | solution.py:40
  208.3 0.0 copy-start.2
  208.3 0.9 copy-done.2
  209.2 6.5 %fusion.7 = bf16[512,3072]{1,0:T(8,128)(2,1)} fusion(bf16[512,768]{1,0:T(8,128)(2,1)S(1)} %fusion.16, bf16[1,3072,768]{2,1,0:T(8,128)(2,1)} %all-gather.4.cloned.1.call-done), kind=kOutput, calls=%fused_computation.11 | convolution fusion | flops 2417491968 | bytes 8650752 | tf_op jit(solution)/shard_map/dot_general | solution.py:40
  215.8 0.0 reduce-scatter.7.cloned.1.call-update
  215.8 0.0 reduce-scatter.9.cloned.1.call-start
  215.9 5.5 %convolution_convert_fusion.1 = bf16[3072,768]{1,0:T(8,128)(2,1)} fusion(bf16[512,3072]{1,0:T(8,128)(2,1)S(1)} %constant_dynamic-update-slice_fusion, bf16[512,768]{1,0:T(8,128)(2,1)} %copy-done.2), kind=kOutput, calls=%fused_computation.3 | convolution fusion | flops 2418278400 | bytes 8650752 | tf_op jit(solution)/shard_map/dot_general | solution.py:46
  221.3 0.0 copy-start.1
  221.3 0.0 reduce-scatter.9.cloned.1.call-update
  221.4 0.0 reduce-scatter.11.cloned.1.call-start
  221.4 2.3 copy-done.1
  223.7 6.4 %convolution_convert_fusion = bf16[768,3072]{1,0:T(8,128)(2,1)} fusion(bf16[512,3072]{1,0:T(8,128)(2,1)S(1)} %copy-done.1, f32[512]{0:T(512)S(1)} %select_reduce_fusion, f32[512,768]{1,0:T(8,128)} %fusion.5), kind=kOutput, calls=%fused_computation.2 | convolution fusion | flops 2426535936 | bytes 9439232 | tf_op jit(solution)/shard_map/dot_general | solution.py:46
  230.1 0.0 reduce-scatter.11.cloned.1.call-update
  230.1 12.1 %reduce-scatter.5.cloned.1.call-done = bf16[128,3072]{1,0:T(8,128)(2,1)} async-done(((bf16[512,3072]{1,0:T(8,128)(2,1)}), bf16[128,3072]{1,0:T(8,128)(2,1)}) %reduce-scatter.5.cloned.1.call-update) | async-done | bytes 786448 | tf_op jit(solution)/shard_map/reduce_scatter | solution.py:77
  242.3 41.1 %reduce-scatter.7.cloned.1.call-done = bf16[128,3072]{1,0:T(8,128)(2,1)} async-done(((bf16[512,3072]{1,0:T(8,128)(2,1)}), bf16[128,3072]{1,0:T(8,128)(2,1)}) %reduce-scatter.7.cloned.1.call-update) | async-done | bytes 786448 | tf_op jit(solution)/shard_map/reduce_scatter | solution.py:79
  283.4 99.5 %reduce-scatter.9.cloned.1.call-done = bf16[384,768]{1,0:T(8,128)(2,1)} async-done(((bf16[3072,768]{1,0:T(8,128)(2,1)}), bf16[384,768]{1,0:T(8,128)(2,1)}) %reduce-scatter.9.cloned.1.call-update) | async-done | bytes 589840 | tf_op jit(solution)/shard_map/reduce_scatter | solution.py:73
  382.9 99.3 %reduce-scatter.11.cloned.1.call-done = bf16[96,3072]{1,0:T(8,128)(2,1)} async-done(((bf16[768,3072]{1,0:T(8,128)(2,1)}), bf16[96,3072]{1,0:T(8,128)(2,1)}) %reduce-scatter.11.cloned.1.call-update) | async-done | bytes 589840 | tf_op jit(solution)/shard_map/reduce_scatter | solution.py:68
  (1 shorter events, 0.0 us)
Async XLA Ops:
  7.2 85.6 %all-gather.4.cloned.1.call-start = ((), (), s32[]{:S(2)}) async-start(), calls=%async_computation.4 | async-start | bytes 5308416 | tf_op jit(solution)/shard_map/all_gather | solution.py:61
  7.9 165.1 %all-gather.6.cloned.1.call-start = ((), (), s32[]{:S(2)}) async-start(), calls=%async_computation.5 | async-start | bytes 5308416 | tf_op jit(solution)/shard_map/all_gather | solution.py:63
  8.6 192.7 %all-gather.8.cloned.1.call-start = ((), (), s32[]{:S(2)}) async-start(), calls=%async_computation.7 | async-start | bytes 3932160 | tf_op jit(solution)/shard_map/all_gather | solution.py:62
  9.4 232.9 %reduce-scatter.5.cloned.1.call-start = ((), (), s32[]{:S(2)}) async-start(), calls=%async_computation.6 | async-start | bytes 3932160 | tf_op jit(solution)/shard_map/reduce_scatter | solution.py:77
  9.4 22.2 %collective-permute-start = (bf16[128,3072]{1,0:T(8,128)(2,1)}, bf16[128,3072]{1,0:T(8,128)(2,1)}, u32[]{:S(2)}, u32[]{:S(2)}) collective-permute-start(bf16[128,3072]{1,0:T(8,128)(2,1)} %param.6), channel_id=1, source_target_pairs={{0,1},{1,2},{2,3},{3,0},{4,5},{5,6},{6,7},{7,4},{8,9},{9,10},{10,1... | collective-permute-start | bytes 2359304 | tf_op jit(solution)/shard_map/ppermute | solution.py:16
  9.9 23.3 %collective-permute-start.1 = (bf16[128,3072]{1,0:T(8,128)(2,1)}, bf16[128,3072]{1,0:T(8,128)(2,1)}, u32[]{:S(2)}, u32[]{:S(2)}) collective-permute-start(bf16[128,3072]{1,0:T(8,128)(2,1)} %param.6), channel_id=1, source_target_pairs={{0,3},{1,0},{2,1},{3,2},{4,7},{5,4},{6,5},{7,6},{8,11},{9,8},{10,9... | collective-permute-start | bytes 2359304 | tf_op jit(solution)/shard_map/ppermute | solution.py:21
  11.9 19.6 %copy-start = (bf16[128,3072]{1,0:T(8,128)(2,1)S(1)}, bf16[128,3072]{1,0:T(8,128)(2,1)}, u32[]{:S(2)}) copy-start(bf16[128,3072]{1,0:T(8,128)(2,1)} %param.6) | copy-start | bytes 2359300
  31.6 12.1 %collective-permute-start.2 = (bf16[128,3072]{1,0:T(8,128)(2,1)}, bf16[128,3072]{1,0:T(8,128)(2,1)S(1)}, u32[]{:S(2)}, u32[]{:S(2)}) collective-permute-start(bf16[128,3072]{1,0:T(8,128)(2,1)} %collective-permute-done), channel_id=1, source_target_pairs={{0,1},{1,2},{2,3},{3,0},{4,5},{5,6},{6,7},{7,4},{8,9},{9,10},{10,1... | collective-permute-start | bytes 2359304 | tf_op jit(solution)/shard_map/ppermute | solution.py:16
  180.3 103.1 %reduce-scatter.7.cloned.1.call-start = ((), (), s32[]{:S(2)}) async-start(), calls=%async_computation.8 | async-start | bytes 3932160 | tf_op jit(solution)/shard_map/reduce_scatter | solution.py:79
  208.3 0.9 copy-start.2
  215.8 167.1 %reduce-scatter.9.cloned.1.call-start = ((), (), s32[]{:S(2)}) async-start(), calls=%async_computation.9 | async-start | bytes 5308416 | tf_op jit(solution)/shard_map/reduce_scatter | solution.py:73
  221.3 2.3 copy-start.1
  221.4 260.8 %reduce-scatter.11.cloned.1.call-start = ((), (), s32[]{:S(2)}) async-start(), calls=%async_computation.10 | async-start | bytes 5308416 | tf_op jit(solution)/shard_map/reduce_scatter | solution.py:68
Sparse Core Ops, SparseCore 0:
  10.2 82.5 all-gather.3
  95.0 78.0 all-gather.5
  174.6 26.6 all-gather.7
  204.3 37.9 reduce-scatter.4
  245.4 37.9 reduce-scatter.6
  287.5 95.4 reduce-scatter.8
  387.1 94.9 reduce-scatter.10
